TPU v7x, 256 devices: a whole 4x4x8 slice. The times are simulated.
256 devices in a mesh: tower: 64 (over x, y, z_hi, core), member: 4 (over z_lo).
Axes of the slice: x: 4, y: 4, z: 8 (z_hi: 2, z_lo: 4; z = z_hi * 4 + z_lo), core: 2. Of those that a mesh axis runs over, the one named last changes fastest.
Arguments:
- slabs: bfloat16 [64, 1024, 4096], P('tower', None, 'member'), may hold values from -6 to 6
- cross_down: bfloat16 [64, 2, 4096, 512], P('tower', None, None, 'member'), may hold values from -0.09375 to 0.09375
- cross_up: bfloat16 [64, 2, 4096, 512], P('tower', None, None, 'member'), may hold values from -0.25 to 0.25
- cross_bias: float32 [64, 2, 4096], P('tower'), may hold values from -3 to 3
- projector: bfloat16 [64, 4096, 256], P('tower'), may hold values from -0.09375 to 0.09375
- placement: int32 [64, 32], P('tower'), may hold values from 0 to 31, each once within a row
- owner: int32 [4, 256], replicated, may hold values from 0 to 255, each once within a row
- inter_grad: bfloat16 [1024, 16384], P(('tower', 'member')), may hold values from -6 to 6
Outputs:
- interactions: float32 [1024, 16384], P(('tower', 'member'))
- slab_grad: bfloat16 [64, 1024, 4096], P('tower', None, 'member')
Inputs may be any that keep to these rules, and one draw needn't show every extreme that they name: Each row of placement names every feature of its tower once. Each row of owner names every sample of its block once.
All inputs are finite; a program needn't handle non-finite values.
Results may differ from a plain program's by a relative error of at most 0.018.
Values may be sent and summed in bfloat16 or wider, within the bound.
A program may use at most 128 MiB of HBM per device.

v0:
```python
import jax
import jax.numpy as jnp
from jax import lax
from jax.sharding import PartitionSpec as P


def side_by_side(arrays, axis, dim, along):
    both = jnp.concatenate(arrays, axis=along)
    filled, at, finished = (lax.all_gather(both, axis, axis=dim, tiled=True), 0, [])
    for a in arrays:
        finished.append(lax.slice_in_dim(filled, at, at + a.shape[along], axis=along))
        at += a.shape[along]
    return tuple(finished)


def per_device(slabs, cross_down, cross_up, cross_bias, projector, placement, owner, inter_grad):
    gathered = lax.all_to_all(slabs, "member", split_axis=1, concat_axis=2, tiled=True)
    row_count = gathered.shape[1]
    full_width = gathered.shape[2]
    features = placement.shape[1]
    slot_width = full_width // features
    depth_count = cross_down.shape[1]
    order = placement[0]
    inputs = (
        gathered[0]
        .reshape(row_count, features, slot_width)[:, order]
        .reshape(row_count, full_width)
    )
    inputs_f = inputs.astype(jnp.float32)
    biases = cross_bias[0]
    whole_down, whole_up = side_by_side((cross_down, cross_up), "member", 3, 0)
    current = inputs
    scales = []
    for depth in range(depth_count):
        hidden = jnp.dot(current, whole_down[0, depth], preferred_element_type=jnp.float32).astype(
            jnp.bfloat16
        )
        scale_now = (
            jnp.dot(hidden, whole_up[0, depth].T, preferred_element_type=jnp.float32)
            + biases[depth]
        )
        scales.append(scale_now)
        current = (inputs_f * scale_now + current.astype(jnp.float32)).astype(jnp.bfloat16)
    vector = jnp.dot(current, projector[0], preferred_element_type=jnp.float32).astype(jnp.bfloat16)
    own_row = lax.dynamic_index_in_dim(owner, lax.axis_index("member"), 0, keepdims=False)
    ordered = vector[own_row]
    owned = lax.all_to_all(ordered[:, None, :], "tower", split_axis=0, concat_axis=1, tiled=True)
    owned_rows = owned.shape[0]
    tower_count = owned.shape[1]
    owned_f = owned.reshape(owned_rows, -1, slot_width).astype(jnp.float32)
    vector_count = owned_f.shape[1]
    table = jnp.einsum("bie,bje->bij", owned_f, owned_f) / slot_width
    interactions = table.reshape(owned_rows, vector_count * vector_count)
    cotangent = inter_grad.astype(jnp.float32).reshape(owned_rows, vector_count, vector_count)
    symmetric = cotangent + jnp.swapaxes(cotangent, 1, 2)
    vec_grad = (jnp.einsum("bij,bje->bie", symmetric, owned_f) / slot_width).astype(jnp.bfloat16)
    vec_grad = vec_grad.reshape(owned_rows, tower_count, -1)
    returned = lax.all_to_all(vec_grad, "tower", split_axis=1, concat_axis=0, tiled=True)
    inverse_own = jnp.argsort(own_row)
    local_grad = returned[:, 0, :][inverse_own]
    gradient = jnp.dot(local_grad, projector[0].T, preferred_element_type=jnp.float32)
    accum = jnp.zeros((row_count, full_width), jnp.float32)
    for depth in reversed(range(depth_count)):
        accum = accum + gradient * scales[depth]
        dscale = (gradient * inputs_f).astype(jnp.bfloat16)
        dhidden = jnp.dot(dscale, whole_up[0, depth], preferred_element_type=jnp.float32).astype(
            jnp.bfloat16
        )
        gradient = gradient + jnp.dot(
            dhidden, whole_down[0, depth].T, preferred_element_type=jnp.float32
        )
    total = (gradient + accum).astype(jnp.bfloat16)
    inverse_place = jnp.argsort(order)
    unplaced = total.reshape(row_count, features, slot_width)[:, inverse_place].reshape(
        1, row_count, full_width
    )
    slab_grad = lax.all_to_all(unplaced, "member", split_axis=2, concat_axis=1, tiled=True)
    return (interactions, slab_grad)


def solution(mesh):
    placed = (
        P("tower", None, "member"),
        P("tower", None, None, "member"),
        P("tower", None, None, "member"),
        P("tower", None, None),
        P("tower", None, None),
        P("tower", None),
        P(),
        P(("tower", "member"), None),
    )
    return jax.shard_map(
        per_device,
        mesh=mesh,
        in_specs=placed,
        out_specs=(P(("tower", "member"), None), P("tower", None, "member")),
        check_vma=False,
    )
```

profile of v0, /device:TPU:1, one launch (start us, length us, event | category | flops | bytes accessed | tf_op | source)
XLA Modules:
  0.0 577.2 jit_solution(18323629134113694175)
XLA Ops:
  7.2 0.0 copy-start
  7.2 0.0 all-gather.2.cloned.1.call-start
  7.2 4.7 pad_maximum_fusion
  11.9 0.0 all-gather.2.cloned.1.call-update
  11.9 6.8 %copy.96 = bf16[1,1024,1024]{2,0,1:T(2,128)(2,1)} copy(bf16[1,1024,1024]{2,1,0:T(8,128)(2,1)} %param.8) | data formatting | bytes 4194304 | tf_op args[0]
  18.7 0.5 broadcast.89
  19.2 14.0 %reduce.1 = bf16[1024,1024]{1,0:T(8,128)(2,1)} reduce(bf16[1024,1,1024]{2,1,0:T(2,128)(2,1)} %bitcast.163, bf16[]{:T(256)} %broadcast.89), dimensions={1}, to_apply=%bitcast.161.reduce_sub_computation | reduce | bytes 4194306
  33.3 0.0 copy-start.5
  33.3 0.0 copy-start.4
  33.3 4.6 reshape.137
  37.9 6.4 %all-to-all-start = ((bf16[4,2,131072]{2,1,0:T(2,128)(2,1)}), bf16[4,2,131072]{2,1,0:T(2,128)(2,1)}, u32[]{:S(2)}, u32[]{:S(2)}) async-start(bf16[4,2,131072]{2,1,0:T(2,128)(2,1)} %reshape.137), calls=%async_computation | async-start | bytes 4194304 | tf_op jit(solution)/shard_map/all_to_all | solution.py:17
  44.3 0.7 compare_select_fusion
  44.9 0.0 copy-done.5
  45.0 0.0 copy-done.4
  45.0 104.7 %all-to-all-done = bf16[4,2,131072]{2,1,0:T(2,128)(2,1)} async-done(((bf16[4,2,131072]{2,1,0:T(2,128)(2,1)}), bf16[4,2,131072]{2,1,0:T(2,128)(2,1)}, u32[]{:S(2)}, u32[]{:S(2)}) %all-to-all-start) | async-done | bytes 2097184 | tf_op jit(solution)/shard_map/all_to_all | solution.py:17
  149.7 5.0 reshape.138
  154.6 4.3 copy.52
  159.0 4.0 copy.41
  162.9 4.1 copy.42
  167.0 3.7 gather_fusion
  170.7 182.7 %all-gather.2.cloned.1.call-done = bf16[2,2,4096,512]{3,2,1,0:T(8,128)(2,1)} async-done(((bf16[2,2,4096,128]{3,2,1,0:T(8,128)(2,1)}), bf16[2,2,4096,512]{3,2,1,0:T(8,128)(2,1)}) %all-gather.2.cloned.1.call-update) | async-done | bytes 16777232 | tf_op jit(solution)/shard_map/all_gather | solution.py:9
  353.5 8.4 %convolution_add_fusion.3 = f32[256,4096]{1,0:T(8,128)} fusion(bf16[2,2,4096,512]{3,2,1,0:T(8,128)(2,1)} %all-gather.2.cloned.1.call-done, f32[4096]{0:T(1024)S(1)} %bitcast.179, bf16[32,256,128]{2,1,0:T(8,128)(2,1)} %gather_fusion), kind=kOutput, calls=%fused_computation.12 | convolution fusion | flops 2148663296 | bytes 14696448 | tf_op jit(solution)/shard_map/dot_general | solution.py:39
  361.9 9.6 %convolution_add_fusion.2 = f32[256,4096]{1,0:T(8,128)} fusion(bf16[2,2,4096,512]{3,2,1,0:T(8,128)(2,1)} %all-gather.2.cloned.1.call-done, f32[4096]{0:T(1024)S(1)} %bitcast.178, f32[256,4096]{1,0:T(8,128)} %convolution_add_fusion.3, bf16[32,256,128]{2,1,0:T(8,128)(2,1)} %gather_fusion), kind=kOutput, calls=%fused_computation.11 | convolution fusion | flops 2152857600 | bytes 18890752 | tf_op jit(solution)/shard_map/dot_general | solution.py:39
  371.5 0.0 copy-done
  371.5 0.0 copy-start.3
  371.5 5.0 fusion.41
  376.5 1.2 gather_fusion.1
  377.7 0.6 reduce.2
  378.3 0.7 reshape.139
  379.0 10.6 %all-to-all-start.1 = ((bf16[64,2,512]{2,1,0:T(2,128)(2,1)}), bf16[64,2,512]{2,1,0:T(2,128)(2,1)S(1)}, u32[]{:S(2)}, u32[]{:S(2)}) async-start(bf16[64,2,512]{2,1,0:T(2,128)(2,1)} %reshape.139), calls=%async_computation.1 | async-start | bytes 262144 | tf_op jit(solution)/shard_map/all_to_all | solution.py:47
  389.6 0.0 copy-done.3
  389.7 0.1 copy.46
  389.8 3.2 sort.34
  393.0 1.6 sort.35
  394.6 7.5 %all-to-all-done.1 = bf16[64,2,512]{2,1,0:T(2,128)(2,1)S(1)} async-done(((bf16[64,2,512]{2,1,0:T(2,128)(2,1)}), bf16[64,2,512]{2,1,0:T(2,128)(2,1)S(1)}, u32[]{:S(2)}, u32[]{:S(2)}) %all-to-all-start.1) | async-done | bytes 131104 | tf_op jit(solution)/shard_map/all_to_all | solution.py:47
  402.1 0.1 reshape.140
  402.2 0.8 reduce
  403.1 0.2 fusion.40
  403.3 0.8 copy.47
  404.1 5.2 all-to-all-start.2
  409.4 12.4 %all-to-all-done.2 = bf16[4,64,256]{2,0,1:T(4,128)(2,1)S(1)} async-done(((bf16[4,64,256]{2,0,1:T(4,128)(2,1)}), bf16[4,64,256]{2,0,1:T(4,128)(2,1)S(1)}, u32[]{:S(2)}, u32[]{:S(2)}) %all-to-all-start.2) | async-done | bytes 131104 | tf_op jit(solution)/shard_map/all_to_all | solution.py:58
  421.9 1.2 gather_fusion.2
  423.0 2.7 fusion.19
  425.7 0.0 copy-start.2
  425.7 10.9 %convolution_add_fusion.1 = f32[256,4096]{1,0:T(8,128)} fusion(f32[256,4096]{1,0:T(8,128)} %fusion.19, bf16[2,2,4096,512]{3,2,1,0:T(8,128)(2,1)} %all-gather.2.cloned.1.call-done, bf16[32,256,128]{2,1,0:T(8,128)(2,1)} %gather_fusion), kind=kOutput, calls=%fused_computation.10 | convolution fusion | flops 2151809024 | bytes 23068672 | tf_op jit(solution)/shard_map/dot_general | solution.py:69
  436.7 0.0 copy-done.2
  436.7 13.5 %fusion.22 = bf16[32,32,8,128]{3,2,1,0:T(8,128)(2,1)} fusion(f32[256,4096]{1,0:T(8,128)} %convolution_add_fusion.1, f32[256,4096]{1,0:T(8,128)} %convolution_add_fusion.3, f32[256,4096]{1,0:T(8,128)} %fusion.19, f32[256,4096]{1,0:T(8,128)} %convolution_add_fusion.2, bf16[2,2,4096,512]{3,2,1,0:T(8,128)(2,1)} %all-gather.2.cloned.1.call-done, ...), kind=kOutput, calls=%fused_computation.38 | convolution fusion | flops 2157051904 | bytes 33554432 | tf_op jit(solution)/shard_map/dot_general | solution.py:69
  450.1 2.2 copy.92
  452.3 2.1 gather_fusion.3
  454.4 3.3 copy.49
  457.7 25.1 %copy.95 = bf16[1,256,4096]{1,0,2:T(2,128)(2,1)} copy(bf16[1,256,4096]{1,2,0:T(8,128)(2,1)S(1)} %bitcast.167) | data formatting | bytes 4194304 | tf_op jit(solution)/shard_map/reshape | solution.py:74
  482.8 21.8 %reduce.3 = bf16[4096,256]{1,0:T(8,128)(2,1)S(1)} reduce(bf16[4096,1,256]{2,1,0:T(2,128)(2,1)} %bitcast.162, bf16[]{:T(256)} %broadcast.89), dimensions={1}, to_apply=%bitcast.160.reduce_sub_computation | reduce | bytes 4194306
  504.6 2.1 reshape.141
  506.6 4.7 all-to-all-start.3
  511.3 0.2 fusion.39
  511.5 0.9 copy.94
  512.4 46.6 %all-to-all-done.3 = bf16[4,2,131072]{2,1,0:T(2,128)(2,1)S(1)} async-done(((bf16[4,2,131072]{2,1,0:T(2,128)(2,1)}), bf16[4,2,131072]{2,1,0:T(2,128)(2,1)S(1)}, u32[]{:S(2)}, u32[]{:S(2)}) %all-to-all-start.3) | async-done | bytes 2097184 | tf_op jit(solution)/shard_map/all_to_all | solution.py:77
  559.0 3.4 reshape.142
  562.4 0.0 copy-start.1
  562.4 4.0 copy.54
  566.4 3.9 copy.51
  570.3 0.0 copy-done.1
  (17 shorter events, 0.3 us)
Async XLA Ops:
  7.2 364.4 %copy-start = (bf16[1,4096,256]{2,1,0:T(8,128)(2,1)S(1)}, bf16[1,4096,256]{2,1,0:T(8,128)(2,1)}, u32[]{:S(2)}) copy-start(bf16[1,4096,256]{2,1,0:T(8,128)(2,1)} %param.12) | copy-start | bytes 6291460
  7.2 346.3 %all-gather.2.cloned.1.call-start = ((), (), s32[]{:S(2)}) async-start(), calls=%async_computation.4 | async-start | bytes 20971520 | tf_op jit(solution)/shard_map/all_gather | solution.py:9
  33.3 11.7 %copy-start.5 = (s32[1,32]{1,0:T(1,128)S(1)}, s32[1,32]{1,0:T(1,128)}, u32[]{:S(2)}) copy-start(s32[1,32]{1,0:T(1,128)} %param.13) | copy-start | bytes 388
  33.3 11.7 %copy-start.4 = (f32[1,2,4096]{2,1,0:T(2,128)S(1)}, f32[1,2,4096]{2,1,0:T(2,128)}, u32[]{:S(2)}) copy-start(f32[1,2,4096]{2,1,0:T(2,128)} %param.11) | copy-start | bytes 98308
  37.9 111.8 %all-to-all-start = ((bf16[4,2,131072]{2,1,0:T(2,128)(2,1)}), bf16[4,2,131072]{2,1,0:T(2,128)(2,1)}, u32[]{:S(2)}, u32[]{:S(2)}) async-start(bf16[4,2,131072]{2,1,0:T(2,128)(2,1)} %reshape.137), calls=%async_computation | async-start | bytes 4194304 | tf_op jit(solution)/shard_map/all_to_all | solution.py:17
  371.5 18.1 %copy-start.3 = (bf16[4,16384]{1,0:T(4,128)(2,1)S(1)}, bf16[4,16384]{1,0:T(4,128)(2,1)}, u32[]{:S(2)}) copy-start(bf16[4,16384]{1,0:T(4,128)(2,1)} %param.15) | copy-start | bytes 393220
  379.0 23.1 %all-to-all-start.1 = ((bf16[64,2,512]{2,1,0:T(2,128)(2,1)}), bf16[64,2,512]{2,1,0:T(2,128)(2,1)S(1)}, u32[]{:S(2)}, u32[]{:S(2)}) async-start(bf16[64,2,512]{2,1,0:T(2,128)(2,1)} %reshape.139), calls=%async_computation.1 | async-start | bytes 262144 | tf_op jit(solution)/shard_map/all_to_all | solution.py:47
  404.1 17.7 %all-to-all-start.2 = ((bf16[4,64,256]{2,0,1:T(4,128)(2,1)}), bf16[4,64,256]{2,0,1:T(4,128)(2,1)S(1)}, u32[]{:S(2)}, u32[]{:S(2)}) async-start(bf16[4,64,256]{2,0,1:T(4,128)(2,1)} %copy.47), calls=%async_computation.2 | async-start | bytes 262144 | tf_op jit(solution)/shard_map/all_to_all | solution.py:58
  425.7 11.0 %copy-start.2 = (bf16[32,256,128]{2,1,0:T(8,128)(2,1)S(1)}, bf16[32,256,128]{2,1,0:T(8,128)(2,1)}, u32[]{:S(2)}) copy-start(bf16[32,256,128]{2,1,0:T(8,128)(2,1)} %gather_fusion) | copy-start | bytes 6291460
  506.6 52.4 %all-to-all-start.3 = ((bf16[4,2,131072]{2,1,0:T(2,128)(2,1)}), bf16[4,2,131072]{2,1,0:T(2,128)(2,1)S(1)}, u32[]{:S(2)}, u32[]{:S(2)}) async-start(bf16[4,2,131072]{2,1,0:T(2,128)(2,1)} %reshape.141), calls=%async_computation.3 | async-start | bytes 4194304 | tf_op jit(solution)/shard_map/all_to_all | solution.py:77
  562.4 8.0 %copy-start.1 = (bf16[1,4096,256]{2,1,0:T(8,128)(2,1)S(1)}, bf16[1,4096,256]{2,1,0:T(8,128)(2,1)}, u32[]{:S(2)}) copy-start(bf16[1,4096,256]{2,1,0:T(8,128)(2,1)} %param.12) | copy-start | bytes 6291460
Sparse Core Ops, SparseCore 0:
  12.0 341.3 all-gather.1
where the time goes:
time: 578 us; the launch traced here: 577 us
  waiting for transfers between devices  354 us (61%)
  local copies, waits for them, and re-layouts  84.1 us (15%)
  matrix products  50.5 us (9%)
  other arithmetic  47.4 us (8%)
  starting transfers between devices  26.9 us (5%)
  between operations  14.3 us (2%)
    all_gather x1, waiting for transfers between devices, side_by_side(): lax.all_gather(both, axis, axis=dim, tiled=True)  183 us
    all_to_all x1, waiting for transfers between devices, per_device(): lax.all_to_all(slabs, 'member', split_axis=1, concat_axis=2, tiled=True)  105 us
    all_to_all x1, waiting for transfers between devices, per_device(): lax.all_to_all(unplaced, 'member', split_axis=2, concat_axis=1, tiled=True)  46.6 us
    unnamed x3, other arithmetic  35.8 us
    unnamed x24, local copies, waits for them, and re-layouts  32.4 us
    reshape x2, local copies, waits for them, and re-layouts, per_device(): total.reshape(row_count, features, slot_width)[:, inverse_place]  27.2 us
    dot_general x2, matrix products, per_device(): jnp.dot(dhidden, whole_down[0, depth].T, preferred_element_type=jnp.float32)  24.4 us
    dot_general x2, matrix products, per_device(): jnp.dot(hidden, whole_up[0, depth].T, preferred_element_type=jnp.float32)  18.1 us
  transfers between devices with their start and end apart: 5, of which 5 were waited for; matrix products, arithmetic and copies ran while one was open for 9% of the time, Pallas kernels for 0%

commit v1 on v0

--- a/solution.py
+++ b/solution.py
@@ -44,7 +44,12 @@
     vector = jnp.dot(current, projector[0], preferred_element_type=jnp.float32).astype(jnp.bfloat16)
     own_row = lax.dynamic_index_in_dim(owner, lax.axis_index("member"), 0, keepdims=False)
     ordered = vector[own_row]
-    owned = lax.all_to_all(ordered[:, None, :], "tower", split_axis=0, concat_axis=1, tiled=True)
+    owned = jnp.concatenate(
+        lax.all_to_all(
+            jnp.stack(jnp.split(ordered[:, None, :], lax.axis_size("tower"), axis=0)), "tower", 0, 0
+        ),
+        axis=1,
+    )
     owned_rows = owned.shape[0]
     tower_count = owned.shape[1]
     owned_f = owned.reshape(owned_rows, -1, slot_width).astype(jnp.float32)

time: 578 us -> 613 us (1.061)
  local copies, waits for them, and re-layouts: 84.1 us -> 120 us
    unnamed x24 -> x85, local copies, waits for them, and re-layouts: 32.4 us -> 68.2 us
where the time goes in v1:
time: 613 us; the launch traced here: 612 us
  waiting for transfers between devices  354 us (58%)
  local copies, waits for them, and re-layouts  120 us (20%)
  matrix products  50.5 us (8%)
  other arithmetic  46 us (8%)
  starting transfers between devices  26.3 us (4%)
  between operations  14.3 us (2%)
    all_gather x1, waiting for transfers between devices, side_by_side(): lax.all_gather(both, axis, axis=dim, tiled=True)  183 us
    all_to_all x1, waiting for transfers between devices, per_device(): lax.all_to_all(slabs, 'member', split_axis=1, concat_axis=2, tiled=True)  103 us
    unnamed x85, local copies, waits for them, and re-layouts  68.2 us
    all_to_all x1, waiting for transfers between devices, per_device(): lax.all_to_all(unplaced, 'member', split_axis=2, concat_axis=1, tiled=True)  46.6 us
    unnamed x3, other arithmetic  35.8 us
    reshape x2, local copies, waits for them, and re-layouts, per_device(): total.reshape(row_count, features, slot_width)[:, inverse_place]  27.2 us
    dot_general x2, matrix products, per_device(): jnp.dot(dhidden, whole_down[0, depth].T, preferred_element_type=jnp.float32)  24.4 us
    dot_general x2, matrix products, per_device(): jnp.dot(hidden, whole_up[0, depth].T, preferred_element_type=jnp.float32)  18.1 us
  transfers between devices with their start and end apart: 5, of which 5 were waited for; matrix products, arithmetic and copies ran while one was open for 9% of the time, Pallas kernels for 0%

profile of v1, /device:TPU:1, one launch (start us, length us, event | category | flops | bytes accessed | tf_op | source)
XLA Modules:
  0.0 611.6 jit_solution(14642055641199190744)
XLA Ops:
  7.2 4.7 pad_maximum_fusion
  11.9 6.8 %copy.82 = bf16[1,1024,1024]{2,0,1:T(2,128)(2,1)} copy(bf16[1,1024,1024]{2,1,0:T(8,128)(2,1)} %param.8) | data formatting | bytes 4194304 | tf_op args[0]
  19.2 14.0 %reduce = bf16[1024,1024]{1,0:T(8,128)(2,1)} reduce(bf16[1024,1,1024]{2,1,0:T(2,128)(2,1)} %bitcast.417, bf16[]{:T(256)} %broadcast.88), dimensions={1}, to_apply=%bitcast.416.reduce_sub_computation | reduce | bytes 4194306
  33.3 4.6 reshape.263
  37.9 6.4 %all-to-all-start = ((bf16[4,2,131072]{2,1,0:T(2,128)(2,1)}), bf16[4,2,131072]{2,1,0:T(2,128)(2,1)}, u32[]{:S(2)}, u32[]{:S(2)}) async-start(bf16[4,2,131072]{2,1,0:T(2,128)(2,1)} %reshape.263), calls=%async_computation | async-start | bytes 4194304 | tf_op jit(solution)/shard_map/all_to_all | solution.py:17
  44.3 1.6 sort.35
  45.9 0.7 compare_select_fusion
  46.6 103.0 %all-to-all-done = bf16[4,2,131072]{2,1,0:T(2,128)(2,1)} async-done(((bf16[4,2,131072]{2,1,0:T(2,128)(2,1)}), bf16[4,2,131072]{2,1,0:T(2,128)(2,1)}, u32[]{:S(2)}, u32[]{:S(2)}) %all-to-all-start) | async-done | bytes 2097184 | tf_op jit(solution)/shard_map/all_to_all | solution.py:17
  149.7 5.0 reshape.264
  154.6 4.3 copy.39
  159.0 4.0 copy.29
  162.9 4.1 copy.30
  167.0 3.7 gather_fusion
  170.7 182.7 %all-gather.2.cloned.1.call-done = bf16[2,2,4096,512]{3,2,1,0:T(8,128)(2,1)} async-done(((bf16[2,2,4096,128]{3,2,1,0:T(8,128)(2,1)}), bf16[2,2,4096,512]{3,2,1,0:T(8,128)(2,1)}) %all-gather.2.cloned.1.call-update) | async-done | bytes 16777232 | tf_op jit(solution)/shard_map/all_gather | solution.py:9
  353.5 8.4 %convolution_add_fusion.3 = f32[256,4096]{1,0:T(8,128)} fusion(bf16[2,2,4096,512]{3,2,1,0:T(8,128)(2,1)} %all-gather.2.cloned.1.call-done, f32[4096]{0:T(1024)S(1)} %bitcast.433, bf16[32,256,128]{2,1,0:T(8,128)(2,1)} %gather_fusion), kind=kOutput, calls=%fused_computation.12 | convolution fusion | flops 2148663296 | bytes 14696448 | tf_op jit(solution)/shard_map/dot_general | solution.py:39
  361.9 9.6 %convolution_add_fusion.2 = f32[256,4096]{1,0:T(8,128)} fusion(bf16[2,2,4096,512]{3,2,1,0:T(8,128)(2,1)} %all-gather.2.cloned.1.call-done, f32[4096]{0:T(1024)S(1)} %bitcast.432, f32[256,4096]{1,0:T(8,128)} %convolution_add_fusion.3, bf16[32,256,128]{2,1,0:T(8,128)(2,1)} %gather_fusion), kind=kOutput, calls=%fused_computation.11 | convolution fusion | flops 2152857600 | bytes 18890752 | tf_op jit(solution)/shard_map/dot_general | solution.py:39
  371.5 5.0 fusion.41
  376.5 1.2 gather_fusion.1
  378.3 0.6 constant_dynamic-update-slice_fusion.62
  379.4 0.6 constant_dynamic-update-slice_fusion.60
  380.6 0.6 constant_dynamic-update-slice_fusion.58
  381.8 0.6 constant_dynamic-update-slice_fusion.56
  382.9 0.6 constant_dynamic-update-slice_fusion.54
  384.1 0.6 constant_dynamic-update-slice_fusion.52
  385.2 0.6 constant_dynamic-update-slice_fusion.50
  386.4 0.6 constant_dynamic-update-slice_fusion.48
  387.6 0.6 constant_dynamic-update-slice_fusion.46
  388.7 0.6 constant_dynamic-update-slice_fusion.44
  389.9 0.6 constant_dynamic-update-slice_fusion.42
  391.1 0.6 constant_dynamic-update-slice_fusion.40
  392.2 0.6 constant_dynamic-update-slice_fusion.38
  393.4 0.6 constant_dynamic-update-slice_fusion.36
  394.6 0.6 constant_dynamic-update-slice_fusion.34
  395.7 0.6 constant_dynamic-update-slice_fusion.32
  396.9 0.6 constant_dynamic-update-slice_fusion.30
  398.0 0.6 constant_dynamic-update-slice_fusion.28
  399.2 0.6 constant_dynamic-update-slice_fusion.26
  400.4 0.6 constant_dynamic-update-slice_fusion.24
  402.7 0.6 constant_dynamic-update-slice_fusion.20
  403.9 0.6 constant_dynamic-update-slice_fusion.18
  408.5 0.6 constant_dynamic-update-slice_fusion.10
  414.3 0.6 constant_dynamic-update-slice_fusion
  414.9 10.6 %all-to-all-start.1 = ((bf16[64,4,1,256]{3,1,2,0:T(4,128)(2,1)}), bf16[64,4,1,256]{3,1,2,0:T(4,128)(2,1)S(1)}, u32[]{:S(2)}, u32[]{:S(2)}) async-start(bf16[64,4,1,256]{3,1,2,0:T(4,128)(2,1)} %constant_dynamic-update-slice_fusion), calls=%async_computation.1 | async-start | bytes 262144 | tf_op jit(solution)/shard_map/all_to_all | solution.py:48
  425.7 3.2 sort.34
  428.9 9.1 %all-to-all-done.1 = bf16[64,4,1,256]{3,1,2,0:T(4,128)(2,1)S(1)} async-done(((bf16[64,4,1,256]{3,1,2,0:T(4,128)(2,1)}), bf16[64,4,1,256]{3,1,2,0:T(4,128)(2,1)S(1)}, u32[]{:S(2)}, u32[]{:S(2)}) %all-to-all-start.1) | async-done | bytes 131104 | tf_op jit(solution)/shard_map/all_to_all | solution.py:48
  438.3 0.8 copy.34
  439.1 4.6 all-to-all-start.2
  443.7 12.5 %all-to-all-done.2 = bf16[4,64,256]{2,0,1:T(4,128)(2,1)S(1)} async-done(((bf16[4,64,256]{2,0,1:T(4,128)(2,1)}), bf16[4,64,256]{2,0,1:T(4,128)(2,1)S(1)}, u32[]{:S(2)}, u32[]{:S(2)}) %all-to-all-start.2) | async-done | bytes 131104 | tf_op jit(solution)/shard_map/all_to_all | solution.py:63
  456.2 1.2 gather_fusion.2
  457.4 2.7 fusion.19
  460.1 10.9 %convolution_add_fusion.1 = f32[256,4096]{1,0:T(8,128)} fusion(f32[256,4096]{1,0:T(8,128)} %fusion.19, bf16[2,2,4096,512]{3,2,1,0:T(8,128)(2,1)} %all-gather.2.cloned.1.call-done, bf16[32,256,128]{2,1,0:T(8,128)(2,1)} %gather_fusion), kind=kOutput, calls=%fused_computation.10 | convolution fusion | flops 2151809024 | bytes 23068672 | tf_op jit(solution)/shard_map/dot_general | solution.py:74
  471.0 13.5 %fusion.22 = bf16[32,32,8,128]{3,2,1,0:T(8,128)(2,1)} fusion(f32[256,4096]{1,0:T(8,128)} %convolution_add_fusion.1, f32[256,4096]{1,0:T(8,128)} %convolution_add_fusion.3, f32[256,4096]{1,0:T(8,128)} %fusion.19, f32[256,4096]{1,0:T(8,128)} %convolution_add_fusion.2, bf16[2,2,4096,512]{3,2,1,0:T(8,128)(2,1)} %all-gather.2.cloned.1.call-done, ...), kind=kOutput, calls=%fused_computation.38 | convolution fusion | flops 2157051904 | bytes 33554432 | tf_op jit(solution)/shard_map/dot_general | solution.py:74
  484.5 2.2 copy.78
  486.7 2.1 gather_fusion.3
  488.8 3.3 copy.36
  492.1 25.1 %copy.81 = bf16[1,256,4096]{1,0,2:T(2,128)(2,1)} copy(bf16[1,256,4096]{1,2,0:T(8,128)(2,1)S(1)} %bitcast.422) | data formatting | bytes 4194304 | tf_op jit(solution)/shard_map/reshape | solution.py:79
  517.1 21.8 %reduce.1 = bf16[4096,256]{1,0:T(8,128)(2,1)S(1)} reduce(bf16[4096,1,256]{2,1,0:T(2,128)(2,1)} %bitcast.418, bf16[]{:T(256)} %broadcast.88), dimensions={1}, to_apply=%bitcast.415.reduce_sub_computation | reduce | bytes 4194306
  538.9 2.1 reshape.265
  541.0 4.8 all-to-all-start.3
  546.0 0.9 copy.80
  546.8 46.6 %all-to-all-done.3 = bf16[4,2,131072]{2,1,0:T(2,128)(2,1)S(1)} async-done(((bf16[4,2,131072]{2,1,0:T(2,128)(2,1)}), bf16[4,2,131072]{2,1,0:T(2,128)(2,1)S(1)}, u32[]{:S(2)}, u32[]{:S(2)}) %all-to-all-start.3) | async-done | bytes 2097184 | tf_op jit(solution)/shard_map/all_to_all | solution.py:82
  593.5 3.4 reshape.266
  596.8 4.0 copy.40
  600.8 3.9 copy.38
  (73 shorter events, 24.6 us)
Async XLA Ops:
  7.2 364.4 %copy-start = (bf16[1,4096,256]{2,1,0:T(8,128)(2,1)S(1)}, bf16[1,4096,256]{2,1,0:T(8,128)(2,1)}, u32[]{:S(2)}) copy-start(bf16[1,4096,256]{2,1,0:T(8,128)(2,1)} %param.12) | copy-start | bytes 6291460
  7.2 346.3 %all-gather.2.cloned.1.call-start = ((), (), s32[]{:S(2)}) async-start(), calls=%async_computation.4 | async-start | bytes 20971520 | tf_op jit(solution)/shard_map/all_gather | solution.py:9
  33.3 11.0 %copy-start.5 = (s32[1,32]{1,0:T(1,128)S(1)}, s32[1,32]{1,0:T(1,128)}, u32[]{:S(2)}) copy-start(s32[1,32]{1,0:T(1,128)} %param.13) | copy-start | bytes 388
  33.3 13.3 %copy-start.4 = (f32[1,2,4096]{2,1,0:T(2,128)S(1)}, f32[1,2,4096]{2,1,0:T(2,128)}, u32[]{:S(2)}) copy-start(f32[1,2,4096]{2,1,0:T(2,128)} %param.11) | copy-start | bytes 98308
  37.9 111.8 %all-to-all-start = ((bf16[4,2,131072]{2,1,0:T(2,128)(2,1)}), bf16[4,2,131072]{2,1,0:T(2,128)(2,1)}, u32[]{:S(2)}, u32[]{:S(2)}) async-start(bf16[4,2,131072]{2,1,0:T(2,128)(2,1)} %reshape.263), calls=%async_computation | async-start | bytes 4194304 | tf_op jit(solution)/shard_map/all_to_all | solution.py:17
  371.5 54.0 %copy-start.3 = (bf16[4,16384]{1,0:T(4,128)(2,1)S(1)}, bf16[4,16384]{1,0:T(4,128)(2,1)}, u32[]{:S(2)}) copy-start(bf16[4,16384]{1,0:T(4,128)(2,1)} %param.15) | copy-start | bytes 393220
  414.9 23.1 %all-to-all-start.1 = ((bf16[64,4,1,256]{3,1,2,0:T(4,128)(2,1)}), bf16[64,4,1,256]{3,1,2,0:T(4,128)(2,1)S(1)}, u32[]{:S(2)}, u32[]{:S(2)}) async-start(bf16[64,4,1,256]{3,1,2,0:T(4,128)(2,1)} %constant_dynamic-update-slice_fusion), calls=%async_computation.1 | async-start | bytes 262144 | tf_op jit(solution)/shard_map/all_to_all | solution.py:48
  439.1 17.1 %all-to-all-start.2 = ((bf16[4,64,256]{2,0,1:T(4,128)(2,1)}), bf16[4,64,256]{2,0,1:T(4,128)(2,1)S(1)}, u32[]{:S(2)}, u32[]{:S(2)}) async-start(bf16[4,64,256]{2,0,1:T(4,128)(2,1)} %copy.34), calls=%async_computation.2 | async-start | bytes 262144 | tf_op jit(solution)/shard_map/all_to_all | solution.py:63
  460.1 11.0 %copy-start.2 = (bf16[32,256,128]{2,1,0:T(8,128)(2,1)S(1)}, bf16[32,256,128]{2,1,0:T(8,128)(2,1)}, u32[]{:S(2)}) copy-start(bf16[32,256,128]{2,1,0:T(8,128)(2,1)} %gather_fusion) | copy-start | bytes 6291460
  541.0 52.5 %all-to-all-start.3 = ((bf16[4,2,131072]{2,1,0:T(2,128)(2,1)}), bf16[4,2,131072]{2,1,0:T(2,128)(2,1)S(1)}, u32[]{:S(2)}, u32[]{:S(2)}) async-start(bf16[4,2,131072]{2,1,0:T(2,128)(2,1)} %reshape.265), calls=%async_computation.3 | async-start | bytes 4194304 | tf_op jit(solution)/shard_map/all_to_all | solution.py:82
  596.8 8.0 %copy-start.1 = (bf16[1,4096,256]{2,1,0:T(8,128)(2,1)S(1)}, bf16[1,4096,256]{2,1,0:T(8,128)(2,1)}, u32[]{:S(2)}) copy-start(bf16[1,4096,256]{2,1,0:T(8,128)(2,1)} %param.12) | copy-start | bytes 6291460
Sparse Core Ops, SparseCore 0:
  12.0 341.3 all-gather.1
